TPU v7x, 256 devices: a whole 4x4x8 slice. The times are simulated.
256 devices in a mesh: tm: 32 (over z_lo, x, core), cells: 8 (over y, z_hi).
Axes of the slice: x: 4, y: 4, z: 8 (z_hi: 2, z_lo: 4; z = z_hi * 4 + z_lo), core: 2. Of those that a mesh axis runs over, the one named last changes fastest.
Arguments:
- hist_bin: int32 [16384, 8192], P('tm', 'cells'), may hold values from 0 to 255
- obs_bin: int32 [16384, 8192], P('tm', 'cells'), may hold values from 0 to 255
- fut_bin: int32 [16384, 8192], P('tm', 'cells'), may hold values from 0 to 255
- region_id: int32 [8192], P('cells'), may hold values from 0 to 127, as said below
- bin_width: float32 [8192], P('cells'), may hold values from 0.005 to 0.05
- bin_offset: float32 [8192], P('cells'), may hold values from -4 to 4
Outputs:
- adjusted: float32 [16384, 8192], P('tm', 'cells')
Inputs may be any that keep to these rules, and one draw needn't show every extreme that they name: `region_id`: every zone of 0 to 127 holds exactly 64 cells.
All inputs are finite; a program needn't handle non-finite values.
Results may differ from a plain program's by a relative error of at most 0.0003.
Values sent between devices are 32-bit elements; how exact they have to be, the bound alone decides.
A program may use at most 64 MiB of HBM per device.

v0:
```python
import math
import jax
import jax.numpy as jnp
from jax import lax
from jax.sharding import PartitionSpec as P

BINS = 256
REGIONS = 128
pool_weight = 0.5


def in_order(blocks, dim):
    blocks = jnp.moveaxis(blocks, 0, dim)
    dims = blocks.shape
    return blocks.reshape(*dims[:dim], dims[dim] * dims[dim + 1], *dims[dim + 2 :])


def copy_for_each(array, axis):
    count = lax.axis_size(axis)
    return lax.all_to_all(
        jnp.broadcast_to(array[None], (count, *array.shape)), axis, 0, 0, tiled=True
    )


def collect(array, axis, dim):
    return in_order(copy_for_each(array, axis), dim)


def tally_bins(stacked, levels):
    series, day_count, cell_count = stacked.shape
    day_block = math.gcd(day_count, max(1, 16384 // cell_count))

    def add_block(turn_index, totals):
        portion = lax.dynamic_slice_in_dim(stacked, turn_index * day_block, day_block, 1)
        matches = (portion[..., None] == levels).astype(jnp.bfloat16)
        return totals + jnp.sum(matches, axis=1, dtype=jnp.float32)

    initial = jnp.zeros((series, cell_count, levels.shape[0]), jnp.float32)
    return lax.fori_loop(0, day_count // day_block, add_block, initial)


def quantile_at(rank_rows, before_rows, pooled_rows):
    ramp_terms = jnp.minimum(
        jnp.maximum(rank_rows[:, :, None] - before_rows[:, None, :], 0.0), pooled_rows[:, None, :]
    )
    return jnp.sum(ramp_terms / jnp.maximum(pooled_rows, 1.0)[:, None, :], axis=2)


def build_table(totals, zone_rows, zone_share, widths, offsets, day_total):
    zone_terms = jnp.einsum(
        "cr,srb->scb",
        zone_rows,
        zone_share,
        precision=lax.Precision.HIGHEST,
        preferred_element_type=jnp.float32,
    )
    pooled = totals + pool_weight * day_total * zone_terms
    bins_total = pooled.shape[2]
    ladder = jnp.arange(bins_total, dtype=jnp.int32)
    upper_mask = (ladder[:, None] <= ladder[None, :]).astype(jnp.float32)
    running = jnp.einsum(
        "scb,bd->scd",
        pooled,
        upper_mask,
        precision=lax.Precision.HIGHEST,
        preferred_element_type=jnp.float32,
    )
    before = running - pooled
    future_rank = before[2] + 0.5 * pooled[2]
    row_count = pooled.shape[1]
    group_size = math.gcd(row_count, 128)
    group_count = row_count // group_size

    def per_group(group_rows):
        rank_rows, obs_before, obs_pooled, hist_before, hist_pooled = group_rows
        return (
            quantile_at(rank_rows, obs_before, obs_pooled),
            quantile_at(rank_rows, hist_before, hist_pooled),
        )

    shaped = (
        future_rank.reshape(group_count, group_size, bins_total),
        before[1].reshape(group_count, group_size, bins_total),
        pooled[1].reshape(group_count, group_size, bins_total),
        before[0].reshape(group_count, group_size, bins_total),
        pooled[0].reshape(group_count, group_size, bins_total),
    )
    quant_obs, quant_hist = lax.map(per_group, shaped)
    quant_obs = quant_obs.reshape(row_count, bins_total)
    quant_hist = quant_hist.reshape(row_count, bins_total)
    centers = (ladder.astype(jnp.float32) + 0.5)[None, :]
    return offsets[:, None] + widths[:, None] * (centers + quant_obs - quant_hist)


def apply_table(fut_bin, lookup, levels):
    day_count, cell_count = fut_bin.shape
    day_block = math.gcd(day_count, max(1, 16384 // cell_count))
    folded = fut_bin.reshape(day_count // day_block, day_block, cell_count)

    def select_rows(bins_rows):
        matches = bins_rows[..., None] == levels
        return jnp.sum(jnp.where(matches, lookup[None], 0.0), axis=2)

    return lax.map(select_rows, folded).reshape(day_count, cell_count)


def body(hist_bin, obs_bin, fut_bin, region_id, bin_width, bin_offset):
    day_count, cell_count = hist_bin.shape
    levels = jnp.arange(BINS, dtype=jnp.int32)
    stacked = jnp.stack([hist_bin, obs_bin, fut_bin])
    totals = tally_bins(stacked, levels)
    zone_rows = (region_id[:, None] == jnp.arange(REGIONS, dtype=jnp.int32)[None, :]).astype(
        jnp.float32
    )
    zone_part = jnp.einsum(
        "cr,scb->srb",
        zone_rows,
        totals,
        precision=lax.Precision.HIGHEST,
        preferred_element_type=jnp.float32,
    )
    zone_counts = lax.psum(zone_part, ("tm", "cells"))
    zone_share = zone_counts / jnp.sum(zone_counts, axis=2, keepdims=True)
    day_total = day_count * lax.axis_size("tm")
    share_rows = lax.psum_scatter(totals, "tm", scatter_dimension=1, tiled=True)
    share_count = share_rows.shape[1]
    first_row = lax.axis_index("tm") * share_count
    share_zones = lax.dynamic_slice_in_dim(zone_rows, first_row, share_count, 0)
    share_widths = lax.dynamic_slice_in_dim(bin_width, first_row, share_count, 0)
    share_offsets = lax.dynamic_slice_in_dim(bin_offset, first_row, share_count, 0)
    partial_table = build_table(
        share_rows, share_zones, zone_share, share_widths, share_offsets, day_total
    )
    lookup = collect(partial_table, "tm", 0)
    return apply_table(fut_bin, lookup, levels)


def solution(mesh):
    placed = (
        P("tm", "cells"),
        P("tm", "cells"),
        P("tm", "cells"),
        P("cells"),
        P("cells"),
        P("cells"),
    )
    return jax.shard_map(
        body, mesh=mesh, in_specs=placed, out_specs=P("tm", "cells"), check_vma=False
    )
```

profile of v0, /device:TPU:1, one launch (start us, length us, event | category | flops | bytes accessed | tf_op | source)
XLA Modules:
  0.0 995.9 jit_solution(16803068548199994457)
XLA Ops:
  7.4 6.6 pad_add_fusion
  14.0 453.7 %while.31 = (s32[]{:T(128)}, f32[3,1024,256]{2,1,0:T(8,128)}, s32[3,512,1024]{2,1,0:T(8,128)}, s32[]{:T(128)}, s32[]{:T(128)}, /*index=5*/s32[]{:T(128)}, s32[]{:T(128)}) while((s32[]{:T(128)}, f32[3,1024,256]{2,1,0:T(8,128)}, s32[3,512,1024]{2,1,0:T(8,128)}, s32[]{:T(128)}, s32[]{:T(128)}, /*index=5*/s32[]{:T(128)}, ...), condition=%wide.region_2.0_spmd.clone, body=%wide.region_0.0_spmd.clone.sunk | while | flops 51118084 | bytes 13172873 | solution.py:39
  15.0 9.3 convert_reduce_fusion.2
  27.3 9.3 convert_reduce_fusion.2
  41.6 9.3 convert_reduce_fusion.2
  55.8 9.3 convert_reduce_fusion.2
  70.0 9.3 convert_reduce_fusion.2
  84.3 9.3 convert_reduce_fusion.2
  98.5 9.3 convert_reduce_fusion.2
  112.7 9.3 convert_reduce_fusion.2
  127.0 9.3 convert_reduce_fusion.2
  141.2 9.3 convert_reduce_fusion.2
  155.5 9.3 convert_reduce_fusion.2
  169.7 9.3 convert_reduce_fusion.2
  183.9 9.3 convert_reduce_fusion.2
  198.2 9.3 convert_reduce_fusion.2
  212.4 9.3 convert_reduce_fusion.2
  226.6 9.3 convert_reduce_fusion.2
  240.9 9.3 convert_reduce_fusion.2
  255.1 9.3 convert_reduce_fusion.2
  269.4 9.3 convert_reduce_fusion.2
  283.6 9.3 convert_reduce_fusion.2
  297.8 9.3 convert_reduce_fusion.2
  312.1 9.3 convert_reduce_fusion.2
  326.3 9.3 convert_reduce_fusion.2
  340.5 9.3 convert_reduce_fusion.2
  354.8 9.3 convert_reduce_fusion.2
  369.0 9.3 convert_reduce_fusion.2
  383.2 9.3 convert_reduce_fusion.2
  397.5 9.3 convert_reduce_fusion.2
  411.7 9.3 convert_reduce_fusion.2
  426.0 9.3 convert_reduce_fusion.2
  440.2 9.3 convert_reduce_fusion.2
  454.4 9.3 convert_reduce_fusion.2
  467.7 5.4 convolution_bitcast_fusion
  475.5 253.2 %all-reduce.2.cloned.1.call-done = f32[3,128,256]{1,2,0:T(8,128)} async-done(((f32[3,128,256]{1,2,0:T(8,128)}), f32[3,128,256]{1,2,0:T(8,128)}) %all-reduce.2.cloned.1.call-update) | async-done | bytes 393232 | tf_op jit(solution)/shard_map/psum | solution.py:122
  736.6 6.3 all-to-all-start
  742.8 26.6 %all-to-all-done = f32[32,32,256]{2,1,0:T(8,128)S(1)} async-done(((f32[32,32,256]{2,1,0:T(8,128)}), f32[32,32,256]{2,1,0:T(8,128)S(1)}, u32[]{:S(2)}, u32[]{:S(2)}) %all-to-all-start) | async-done | bytes 1048608 | tf_op jit(solution)/shard_map/all_to_all | solution.py:20
  769.5 219.0 %while.30 = (s32[]{:T(128)}, f32[32,16,1024]{2,1,0:T(8,128)}, s32[32,16,1024]{2,1,0:T(8,128)}, f32[32,32,256]{2,1,0:T(8,128)S(1)}, s32[]{:T(128)}) while((s32[]{:T(128)}, f32[32,16,1024]{2,1,0:T(8,128)}, s32[32,16,1024]{2,1,0:T(8,128)}, f32[32,32,256]{2,1,0:T(8,128)S(1)}, s32[]{:T(128)}) %tuple.66), condition=%wide.region_10.11_spmd.clone, body=%wide.region_8.10_spmd.clone.sunk | while | flops 12566530 | bytes 1442369 | solution.py:104
  770.3 5.3 select_reduce_fusion.2
  777.2 5.3 select_reduce_fusion.2
  784.0 5.3 select_reduce_fusion.2
  790.8 5.3 select_reduce_fusion.2
  797.7 5.3 select_reduce_fusion.2
  804.5 5.3 select_reduce_fusion.2
  811.4 5.3 select_reduce_fusion.2
  818.2 5.3 select_reduce_fusion.2
  825.1 5.3 select_reduce_fusion.2
  (172 shorter events, 337.0 us)
Async XLA Ops:
  7.4 721.3 %all-reduce.2.cloned.1.call-start = ((), (), s32[]{:S(2)}) async-start(), calls=%async_computation.3 | async-start | bytes 786432 | tf_op jit(solution)/shard_map/psum | solution.py:122
  14.0 453.7 %copy-start = (s32[1024]{0:T(1024)S(1)}, s32[1024]{0:T(1024)}, u32[]{:S(2)}) copy-start(s32[1024]{0:T(1024)} %param.13) | copy-start | bytes 12292
  473.2 256.6 %reduce-scatter.2.cloned.1.call-start = ((), (), s32[]{:S(2)}) async-start(), calls=%async_computation.2 | async-start | bytes 3244032 | tf_op jit(solution)/shard_map/reduce_scatter | solution.py:125
  736.6 32.9 %all-to-all-start = ((f32[32,32,256]{2,1,0:T(8,128)}), f32[32,32,256]{2,1,0:T(8,128)S(1)}, u32[]{:S(2)}, u32[]{:S(2)}) async-start(f32[32,32,256]{2,1,0:T(8,128)} %broadcast_in_dim.68), calls=%async_computation.1 | async-start | bytes 2097152 | tf_op jit(solution)/shard_map/all_to_all | solution.py:20
Sparse Core Ops, SparseCore 0:
  473.3 255.3 all-reduce.1
Sparse Core Ops, SparseCore 1:
  476.2 149.1 reduce-scatter.1
where the time goes:
time: 1000 us; the launch traced here: 996 us
  other arithmetic  606 us (61%)
  waiting for transfers between devices  280 us (28%)
  local copies, waits for them, and re-layouts  80.2 us (8%)
  between operations  14.9 us (1%)
    reduce_sum x32, other arithmetic, add_block(): return totals + jnp.sum(matches, axis=1, dtype=jnp.float32)  297 us
    psum x1, waiting for transfers between devices, body(): zone_counts = lax.psum(zone_part, ('tm', 'cells'))  253 us
    reduce_sum x32, other arithmetic, select_rows(): return jnp.sum(jnp.where(matches, lookup[None], 0.0), axis=2)  171 us
    add x32, other arithmetic, add_block(): return totals + jnp.sum(matches, axis=1, dtype=jnp.float32)  126 us
    dynamic_slice x32, local copies, waits for them, and re-layouts, add_block(): lax.dynamic_slice_in_dim(stacked, turn_index * day_block, day_block, 1)  30.1 us
    eq x32, local copies, waits for them, and re-layouts, select_rows(): matches = bins_rows[..., None] == levels  27 us
    all_to_all x1, waiting for transfers between devices, copy_for_each(): lax.all_to_all(jnp.broadcast_to(array[None], (count, *array.shape)), axis...  26.6 us
    dynamic_update_slice x32, local copies, waits for them, and re-layouts, apply_table(): return lax.map(select_rows, folded).reshape(day_count, cell_count)  20.5 us
  transfers between devices with their start and end apart: 3, of which 2 were waited for; matrix products, arithmetic and copies ran while one was open for 0% of the time, Pallas kernels for 0%

commit v1 on v0

--- a/solution.py
+++ b/solution.py
@@ -3,6 +3,7 @@
 import jax.numpy as jnp
 from jax import lax
 from jax.sharding import PartitionSpec as P
+from jax.lax import psum
 
 BINS = 256
 REGIONS = 128
@@ -119,7 +120,7 @@
         precision=lax.Precision.HIGHEST,
         preferred_element_type=jnp.float32,
     )
-    zone_counts = lax.psum(zone_part, ("tm", "cells"))
+    zone_counts = psum(psum(zone_part, "tm"), "cells")
     zone_share = zone_counts / jnp.sum(zone_counts, axis=2, keepdims=True)
     day_total = day_count * lax.axis_size("tm")
     share_rows = lax.psum_scatter(totals, "tm", scatter_dimension=1, tiled=True)

time: 1000 us -> 1280 us (1.28)
  waiting for transfers between devices: 280 us -> 550 us
    reduce_scatter x1, waiting for transfers between devices: 0.02 us -> 147 us  [body(): share_rows = lax.psum_scatter(totals, 'tm', scatter_dimension=1, tiled=True)]
    psum x1 -> x2, waiting for transfers between devices: 253 us -> 375 us  [body(): zone_counts = psum(psum(zone_part, 'tm'), 'cells')]
  transfers between devices with their start and end apart: 3 -> 4, of which waited for: 2 -> 4; matrix products, arithmetic and copies ran while one was open for 0% -> 0% of each run, Pallas kernels for 0% -> 0%
where the time goes in v1:
time: 1280 us; the launch traced here: 1270 us
  other arithmetic  613 us (48%)
  waiting for transfers between devices  550 us (43%)
  local copies, waits for them, and re-layouts  80.2 us (6%)
  between operations  13.2 us (1%)
    psum x2, waiting for transfers between devices, body(): zone_counts = psum(psum(zone_part, 'tm'), 'cells')  375 us
    reduce_sum x32, other arithmetic, add_block(): return totals + jnp.sum(matches, axis=1, dtype=jnp.float32)  297 us
    reduce_sum x32, other arithmetic, select_rows(): return jnp.sum(jnp.where(matches, lookup[None], 0.0), axis=2)  171 us
    reduce_scatter x1, waiting for transfers between devices, body(): share_rows = lax.psum_scatter(totals, 'tm', scatter_dimension=1, tiled=True)  147 us
    add x32, other arithmetic, add_block(): return totals + jnp.sum(matches, axis=1, dtype=jnp.float32)  133 us
    dynamic_slice x32, local copies, waits for them, and re-layouts, add_block(): lax.dynamic_slice_in_dim(stacked, turn_index * day_block, day_block, 1)  30.1 us
    eq x32, local copies, waits for them, and re-layouts, select_rows(): matches = bins_rows[..., None] == levels  27 us
    all_to_all x1, waiting for transfers between devices, copy_for_each(): lax.all_to_all(jnp.broadcast_to(array[None], (count, *array.shape)), axis...  26.8 us
  transfers between devices with their start and end apart: 4, of which 4 were waited for; matrix products, arithmetic and copies ran while one was open for 0% of the time, Pallas kernels for 0%

profile of v1, /device:TPU:1, one launch (start us, length us, event | category | flops | bytes accessed | tf_op | source)
XLA Modules:
  0.0 1273.0 jit_solution(15690752508557590470)
XLA Ops:
  6.5 6.6 pad_add_fusion
  13.2 460.2 %while.31 = (s32[]{:T(128)}, f32[3,1024,256]{2,1,0:T(8,128)}, s32[3,512,1024]{2,1,0:T(8,128)}, s32[]{:T(128)}, s32[]{:T(128)}, /*index=5*/s32[]{:T(128)}, s32[]{:T(128)}) while((s32[]{:T(128)}, f32[3,1024,256]{2,1,0:T(8,128)}, s32[3,512,1024]{2,1,0:T(8,128)}, s32[]{:T(128)}, s32[]{:T(128)}, /*index=5*/s32[]{:T(128)}, ...), condition=%wide.region_2.0_spmd.clone, body=%wide.region_0.0_spmd.clone.sunk | while | flops 51118084 | bytes 13172873 | solution.py:40
  14.1 9.3 convert_reduce_fusion.2
  26.7 9.3 convert_reduce_fusion.2
  41.1 9.3 convert_reduce_fusion.2
  55.6 9.3 convert_reduce_fusion.2
  70.0 9.3 convert_reduce_fusion.2
  84.4 9.3 convert_reduce_fusion.2
  98.9 9.3 convert_reduce_fusion.2
  113.3 9.3 convert_reduce_fusion.2
  127.8 9.3 convert_reduce_fusion.2
  142.2 9.3 convert_reduce_fusion.2
  156.6 9.3 convert_reduce_fusion.2
  171.1 9.3 convert_reduce_fusion.2
  185.5 9.3 convert_reduce_fusion.2
  200.0 9.3 convert_reduce_fusion.2
  214.4 9.3 convert_reduce_fusion.2
  228.8 9.3 convert_reduce_fusion.2
  243.3 9.3 convert_reduce_fusion.2
  257.7 9.3 convert_reduce_fusion.2
  272.1 9.3 convert_reduce_fusion.2
  286.6 9.3 convert_reduce_fusion.2
  301.0 9.3 convert_reduce_fusion.2
  315.5 9.3 convert_reduce_fusion.2
  329.9 9.3 convert_reduce_fusion.2
  344.3 9.3 convert_reduce_fusion.2
  358.8 9.3 convert_reduce_fusion.2
  373.2 9.3 convert_reduce_fusion.2
  387.7 9.3 convert_reduce_fusion.2
  402.1 9.3 convert_reduce_fusion.2
  416.5 9.3 convert_reduce_fusion.2
  431.0 9.3 convert_reduce_fusion.2
  445.4 9.3 convert_reduce_fusion.2
  459.8 9.3 convert_reduce_fusion.2
  473.3 5.4 convolution_bitcast_fusion
  478.8 270.5 %all-reduce.3.cloned.1.call-done = f32[3,128,256]{1,2,0:T(8,128)} async-done(((f32[3,128,256]{1,2,0:T(8,128)}), f32[3,128,256]{1,2,0:T(8,128)}) %all-reduce.3.cloned.1.call-update) | async-done | bytes 393232 | tf_op jit(solution)/shard_map/psum | solution.py:123
  751.8 105.0 %all-reduce.5.cloned.1.call-done = f32[3,128,256]{1,2,0:T(8,128)} async-done(((f32[3,128,256]{1,2,0:T(8,128)}), f32[3,128,256]{1,2,0:T(8,128)}) %all-reduce.5.cloned.1.call-update) | async-done | bytes 393232 | tf_op jit(solution)/shard_map/psum | solution.py:123
  857.8 146.6 %reduce-scatter.2.cloned.1.call-done = f32[3,32,256]{2,1,0:T(8,128)} async-done(((f32[3,1024,256]{2,1,0:T(8,128)}), f32[3,32,256]{2,1,0:T(8,128)}) %reduce-scatter.2.cloned.1.call-update) | async-done | bytes 98320 | tf_op jit(solution)/shard_map/reduce_scatter | solution.py:126
  1011.2 9.4 all-to-all-start
  1020.7 26.8 %all-to-all-done = f32[32,32,256]{2,1,0:T(8,128)S(1)} async-done(((f32[32,32,256]{2,1,0:T(8,128)}), f32[32,32,256]{2,1,0:T(8,128)S(1)}, u32[]{:S(2)}, u32[]{:S(2)}) %all-to-all-start) | async-done | bytes 1048608 | tf_op jit(solution)/shard_map/all_to_all | solution.py:21
  1047.4 219.0 %while.30 = (s32[]{:T(128)}, f32[32,16,1024]{2,1,0:T(8,128)}, s32[32,16,1024]{2,1,0:T(8,128)}, f32[32,32,256]{2,1,0:T(8,128)S(1)}, s32[]{:T(128)}) while((s32[]{:T(128)}, f32[32,16,1024]{2,1,0:T(8,128)}, s32[32,16,1024]{2,1,0:T(8,128)}, f32[32,32,256]{2,1,0:T(8,128)S(1)}, s32[]{:T(128)}) %tuple.68), condition=%wide.region_11.12_spmd.clone, body=%wide.region_9.11_spmd.clone.sunk | while | flops 12566530 | bytes 1442369 | solution.py:105
  1048.3 5.3 select_reduce_fusion.2
  1055.1 5.3 select_reduce_fusion.2
  1062.0 5.3 select_reduce_fusion.2
  1068.8 5.3 select_reduce_fusion.2
  1075.7 5.3 select_reduce_fusion.2
  1082.5 5.3 select_reduce_fusion.2
  1089.3 5.3 select_reduce_fusion.2
  (175 shorter events, 354.3 us)
Async XLA Ops:
  6.5 742.7 %all-reduce.3.cloned.1.call-start = ((), (), s32[]{:S(2)}) async-start(), calls=%async_computation.3 | async-start | bytes 786432 | tf_op jit(solution)/shard_map/psum | solution.py:123
  13.2 460.2 %copy-start = (s32[1024]{0:T(1024)S(1)}, s32[1024]{0:T(1024)}, u32[]{:S(2)}) copy-start(s32[1024]{0:T(1024)} %param.13) | copy-start | bytes 12292
  478.8 378.0 %all-reduce.5.cloned.1.call-start = ((), (), s32[]{:S(2)}) async-start(), calls=%async_computation.4 | async-start | bytes 786432 | tf_op jit(solution)/shard_map/psum | solution.py:123
  749.3 255.1 %reduce-scatter.2.cloned.1.call-start = ((), (), s32[]{:S(2)}) async-start(), calls=%async_computation.2 | async-start | bytes 3244032 | tf_op jit(solution)/shard_map/reduce_scatter | solution.py:126
  1011.2 36.2 %all-to-all-start = ((f32[32,32,256]{2,1,0:T(8,128)}), f32[32,32,256]{2,1,0:T(8,128)S(1)}, u32[]{:S(2)}, u32[]{:S(2)}) async-start(f32[32,32,256]{2,1,0:T(8,128)} %broadcast_in_dim.68), calls=%async_computation.1 | async-start | bytes 2097152 | tf_op jit(solution)/shard_map/all_to_all | solution.py:21
Sparse Core Ops, SparseCore 0:
  478.9 270.3 all-reduce.2
  751.9 104.8 all-reduce.4
  859.3 145.0 reduce-scatter.1
